TPU v7x, 32 devices: a whole 2x2x4 slice. The times are simulated.
32 devices in a mesh: band: 8 (over y, x, core), cols: 4 (over z).
Axes of the slice: x: 2, y: 2, z: 4, core: 2. Of those that a mesh axis runs over, the one named last changes fastest.
Arguments:
- band_diagonals: float32 [256, 3072], P('cols', 'band'), may hold values from -0.4 to 0.4, as said below
- eigenvectors: float32 [3072, 512], P('band', 'cols'), may hold values from -4 to 4
Outputs:
- band_result: float32 [256, 3072], P('cols', 'band')
- transformed: float32 [3072, 512], P('band', 'cols')
Inputs may be any that keep to these rules, and one draw needn't show every extreme that they name: `band_diagonals`: entry [k, r] is the matrix's entry in row r and column r - k; it is zero where k > 128 or r < k.
All inputs are finite; a program needn't handle non-finite values.
Results may differ from a plain program's by a relative error of at most 0.0003.
Values sent between devices are 32-bit elements; how exact they have to be, the bound alone decides.
A program may use at most 64 MiB of HBM per device.

v0:
```python
import jax
import jax.numpy as jnp
from jax import lax
from jax.sharding import PartitionSpec as P

SWEEPS = 4


HIGHEST = lax.Precision.HIGHEST


def padded_2(x, sides, width):
    for axis, dim in sides:
        peers, length = (lax.axis_size(axis), x.shape[dim])
        up = [(i, (i + 1) % peers) for i in range(peers - 1)]
        down = [(j, i) for i, j in up]
        last = lax.slice_in_dim(x, length - width, length, axis=dim)
        first = lax.slice_in_dim(x, 0, width, axis=dim)
        before = lax.ppermute(last, axis, up)
        after = lax.ppermute(first, axis, down)
        x = jnp.concatenate([before, x, after], axis=dim)
    return x


def from_behind(x, axis, by):
    peers = lax.axis_size(axis)
    pairs = [(i, i + by) for i in range(peers) if 0 <= i + by < peers]
    return lax.ppermute(x, axis, pairs)


def skew_rows(block_rows):
    row_count, col_count = block_rows.shape
    flipped = block_rows[:, ::-1]
    padded = jnp.pad(flipped, ((0, 0), (0, row_count)))
    flat_cells = padded.reshape(-1)[: row_count * (col_count + row_count - 1)]
    return flat_cells.reshape(row_count, col_count + row_count - 1)


def unskew_rows(dense_rows, col_count):
    row_count = dense_rows.shape[0]
    flat_cells = jnp.pad(dense_rows.reshape(-1), (0, row_count))
    grid_cells = flat_cells.reshape(row_count, col_count + row_count)
    return grid_cells[:, :col_count][:, ::-1]


def chase_step(region, first_step):
    double = region.shape[0]
    half_width = double // 2
    dense_rows = skew_rows(region)
    offset = half_width - 1
    upper_rows = dense_rows[:half_width, offset : offset + double]
    lower_rows = dense_rows[half_width:, offset + half_width : offset + double]
    left_part = upper_rows[:, :half_width]
    window = upper_rows[:, half_width:]
    column = jnp.where(first_step, left_part[:, half_width - 1], left_part[:, 0])
    length = jnp.sqrt(jnp.sum(column * column))
    vector = column.at[0].add(length)
    factor = 2.0 / jnp.sum(vector * vector)
    mirror = window + window.T - jnp.diag(jnp.diag(window))
    across = factor * jnp.dot(vector, left_part, precision=HIGHEST)
    inside = factor * jnp.dot(mirror, vector, precision=HIGHEST)
    beneath = factor * jnp.dot(lower_rows, vector, precision=HIGHEST)
    inside = inside - 0.5 * factor * jnp.dot(vector, inside, precision=HIGHEST) * vector
    left_part = left_part - vector[:, None] * across[None, :]
    window = window - jnp.tril(
        vector[:, None] * inside[None, :] + inside[:, None] * vector[None, :]
    )
    lower_rows = lower_rows - beneath[:, None] * vector[None, :]
    cleared = jnp.zeros_like(column).at[0].set(-length)
    left_part = jnp.where(
        first_step, left_part.at[:, half_width - 1].set(cleared), left_part.at[:, 0].set(cleared)
    )
    dense_rows = dense_rows.at[:half_width, offset : offset + double].set(
        jnp.concatenate([left_part, window], 1)
    )
    dense_rows = dense_rows.at[half_width:, offset + half_width : offset + double].set(lower_rows)
    return (unskew_rows(dense_rows, double), vector, factor)


def section_active(device, section_index, sweeps):
    offset = section_index - device
    return (offset >= 0) & (offset % 2 == 0) & (offset < 2 * sweeps)


def keep_same(operand):
    return operand


def body(band_diagonals, eigenvectors):
    pieces = lax.all_gather(band_diagonals, "cols", axis=0, tiled=True)
    own_rows = pieces.T
    rows_dev = own_rows.shape[0]
    double = own_rows.shape[1]
    half_width = double // 2
    blocks_dev = rows_dev // half_width
    columns = eigenvectors.shape[1]
    devices = lax.axis_size("band")
    device = lax.axis_index("band")
    sweeps = SWEEPS
    depth = half_width + sweeps
    state = jnp.concatenate([own_rows, jnp.zeros((double, double), jnp.float32)], 0)
    vectors = jnp.zeros((sweeps, blocks_dev, half_width), jnp.float32)
    factors = jnp.zeros((sweeps, blocks_dev), jnp.float32)
    local_steps = jnp.where(device == devices - 1, blocks_dev - 2, blocks_dev)
    sections = 2 * (sweeps - 1) + devices

    def run_sweep(operand):
        state, vectors, factors, sweep_index = operand

        def advance(step_index, carry):

            def apply_step(inner):
                state, vec_rows, tau_row = inner
                anchor = sweep_index + 1 + step_index * half_width
                region = lax.dynamic_slice_in_dim(state, anchor, double, 0)
                first_step = (device == 0) & (step_index == 0)
                region, vector, factor = chase_step(region, first_step)
                state = lax.dynamic_update_slice_in_dim(state, region, anchor, 0)
                vec_rows = vec_rows.at[step_index].set(vector)
                tau_row = tau_row.at[step_index].set(factor)
                return (state, vec_rows, tau_row)

            return lax.cond(step_index < local_steps, apply_step, keep_same, carry)

        vec_rows = jnp.zeros((blocks_dev, half_width), jnp.float32)
        tau_row = jnp.zeros((blocks_dev,), jnp.float32)
        state, vec_rows, tau_row = lax.fori_loop(0, blocks_dev, advance, (state, vec_rows, tau_row))
        vectors = lax.dynamic_update_slice_in_dim(vectors, vec_rows[None], sweep_index, 0)
        factors = lax.dynamic_update_slice_in_dim(factors, tau_row[None], sweep_index, 0)
        return (state, vectors, factors, sweep_index)

    def section(section_index, carry):
        state, vectors, factors = carry
        outgoing = jnp.concatenate([state[:depth], state[rows_dev : rows_dev + depth]], 0)
        padded = padded_2(outgoing, (("band", 0),), depth)
        from_prev = padded[:depth]
        from_next = padded[3 * depth :]
        take_prev = (device > 0) & section_active(device - 1, section_index - 1, sweeps)
        take_next = (section_index == 0) | section_active(device + 1, section_index - 1, sweeps)
        state = state.at[:depth].set(jnp.where(take_prev, from_prev, state[:depth]))
        state = state.at[rows_dev : rows_dev + depth].set(
            jnp.where(take_next, from_next, state[rows_dev : rows_dev + depth])
        )
        busy = section_active(device, section_index, sweeps)
        sweep_index = jnp.clip((section_index - device) // 2, 0, sweeps - 1)
        outcome = lax.cond(busy, run_sweep, keep_same, (state, vectors, factors, sweep_index))
        return (outcome[0], outcome[1], outcome[2])

    state, vectors, factors = lax.fori_loop(0, sections + 1, section, (state, vectors, factors))
    piece_count = band_diagonals.shape[0]
    band_slice = lax.dynamic_slice_in_dim(
        state[:rows_dev].T, lax.axis_index("cols") * piece_count, piece_count, 0
    )
    result = eigenvectors
    for sweep_number in reversed(range(sweeps)):
        vec_rows = vectors[sweep_number]
        tau_row = factors[sweep_number]
        lead_rows = sweep_number + 1
        fetched = from_behind(result[:half_width], "band", -1)
        extended = jnp.concatenate([result, fetched], 0)
        blocks = extended[lead_rows : lead_rows + rows_dev].reshape(blocks_dev, half_width, columns)
        inner_sums = jnp.einsum("kb,kbc->kc", vec_rows, blocks, precision=HIGHEST)
        blocks = blocks - (tau_row[:, None] * vec_rows)[:, :, None] * inner_sums[:, None, :]
        extended = extended.at[lead_rows : lead_rows + rows_dev].set(
            blocks.reshape(rows_dev, columns)
        )
        returned = from_behind(extended[rows_dev:], "band", 1)
        replace = (lax.broadcasted_iota(jnp.int32, (half_width, 1), 0) < lead_rows) & (device > 0)
        head_rows = jnp.where(replace, returned, extended[:half_width])
        result = jnp.concatenate([head_rows, extended[half_width:rows_dev]], 0)
    return (band_slice, result)


def solution(mesh):
    return jax.shard_map(
        body,
        mesh=mesh,
        in_specs=(P("cols", "band"), P("band", "cols")),
        out_specs=(P("cols", "band"), P("band", "cols")),
        check_vma=False,
    )
```

profile of v0, /device:TPU:25, one launch (start us, length us, event | category | flops | bytes accessed | tf_op | source)
XLA Modules:
  0.0 1234.7 jit_solution(14261148486310575008)
XLA Ops:
  4.1 13.4 %all_gather.3 = f32[256,384]{1,0:T(8,128)S(1)} all-gather(f32[64,384]{1,0:T(8,128)S(1)} %copy-done.3), channel_id=1, replica_groups=mesh['band'=8,'cols'=4] {'cols'}, dimensions={0}, use_global_device_ids=true | all-gather | bytes 491520 | tf_op jit(solution)/shard_map/all_gather | solution.py:90
  17.7 1080.8 %while.55 = (s32[]{:T(128)}, f32[640,256]{1,0:T(8,128)S(1)}, f32[4,3,128]{2,1,0:T(4,128)S(1)}, f32[4,3]{1,0:T(4,128)S(1)}, s32[]{:T(128)}, /*index=5*/s32[]{:T(1...) while((s32[]{:T(128)}, f32[640,256]{1,0:T(8,128)S(1)}, ...), condition=%wide.region_12.13_spmd, body=%wide.region_0.12_spmd.sunk | while | flops 971127 | bytes 14984969 | solution.py:149
  17.8 5.3 collective-permute-start
  35.3 71.6 %collective-permute-done = f32[132,256]{1,0:T(8,128)S(1)} collective-permute-done((f32[132,256]{1,0:T(8,128)S(1)}, f32[132,256]{1,0:T(8,128)S(1)}, u32[]{:S(2)}, u32[]{:S(2)}) %collective-permute-start) | collective-permute-done | bytes 135200 | tf_op jit(solution)/shard_map/while/body/eval_jaxpr/ppermute | solution.py:19
  114.3 75.2 %conditional.4 = ((f32[640,256]{1,0:T(8,128)S(1)}, f32[4,3,128]{2,1,0:T(4,128)S(1)}, f32[4,3]{1,0:T(4,128)S(1)})) conditional(s32[]{:T(128)} %convert_element_type.24, (f32[640,256]{1,0:T(8,128)S(1)}, f32[4,3,128]{2,1,0:T(4,128)S(1)}, f32[4,3]{1,0:T(4,128)S(1)}) %tuple.183, (s32[]{:T(128)}, s32[]{:T(128)}, pred[]{:T(512)}, s32[]{:T(128)}, s32[]{:T(128)}, ...), branch_computations={%region_1.1_spmd, %region_2.11_spmd} | conditional | flops 903485 | bytes 12145628 | solution.py:146
  114.4 75.1 %while.54 = (s32[]{:T(128)}, f32[640,256]{1,0:T(8,128)S(1)}, f32[3,128]{1,0:T(4,128)S(1)}, f32[3]{0:T(128)S(1)}, s32[]{:T(128)}, /*index=5*/s32[]{:T(128)}, s32[]{:T(128)}, s32[]{:T(128)}) while((s32[]{:T(128)}, f32[640,256]{1,0:T(8,128)S(1)}, f32[3,128]{1,0:T(4,128)S(1)}, f32[3]{0:T(128)S(1)}, s32[]{:T(128)}, /*index=5*/s32[]{:T(128)}, ...), condition=%wide.region_11.10_spmd, body=%wide.region_3.0_spmd.sunk | while | flops 903471 | bytes 12139696 | solution.py:127
  114.4 25.2 %conditional.5 = ((f32[640,256]{1,0:T(8,128)S(1)}, f32[3,128]{1,0:T(4,128)S(1)}, f32[3]{0:T(128)S(1)})) conditional(s32[]{:T(128)} %convert_element_type.25, (f32[640,256]{1,0:T(8,128)S(1)}, f32[3,128]{1,0:T(4,128)S(1)}, f32[3]{0:T(128)S(1)}) %tuple.186, (s32[]{:T(128)}, s32[]{:T(128)}, f32[640,256]{1,0:T(8,128)S(1)}, s32[]{:T(128)}, ...), branch_computations={%region_4.2_spmd, %region_5.8_spmd} | conditional | flops 903467 | bytes 12139525 | solution.py:123
  129.8 4.4 scatter.26
  139.6 25.2 %conditional.5 = ((f32[640,256]{1,0:T(8,128)S(1)}, f32[3,128]{1,0:T(4,128)S(1)}, f32[3]{0:T(128)S(1)})) conditional(s32[]{:T(128)} %convert_element_type.25, (f32[640,256]{1,0:T(8,128)S(1)}, f32[3,128]{1,0:T(4,128)S(1)}, f32[3]{0:T(128)S(1)}) %tuple.186, (s32[]{:T(128)}, s32[]{:T(128)}, f32[640,256]{1,0:T(8,128)S(1)}, s32[]{:T(128)}, ...), branch_computations={%region_4.2_spmd, %region_5.8_spmd} | conditional | flops 903467 | bytes 12139525 | solution.py:123
  155.0 4.4 scatter.26
  164.7 24.8 %conditional.5 = ((f32[640,256]{1,0:T(8,128)S(1)}, f32[3,128]{1,0:T(4,128)S(1)}, f32[3]{0:T(128)S(1)})) conditional(s32[]{:T(128)} %convert_element_type.25, (f32[640,256]{1,0:T(8,128)S(1)}, f32[3,128]{1,0:T(4,128)S(1)}, f32[3]{0:T(128)S(1)}) %tuple.186, (s32[]{:T(128)}, s32[]{:T(128)}, f32[640,256]{1,0:T(8,128)S(1)}, s32[]{:T(128)}, ...), branch_computations={%region_4.2_spmd, %region_5.8_spmd} | conditional | flops 903467 | bytes 12139525 | solution.py:123
  180.1 4.4 scatter.26
  201.7 77.0 %collective-permute-start = (f32[132,256]{1,0:T(8,128)S(1)}, f32[132,256]{1,0:T(8,128)S(1)}, u32[]{:S(2)}, u32[]{:S(2)}) collective-permute-start(f32[132,256]{1,0:T(8,128)S(1)} %slice.505), channel_id=1, source_target_pairs={{0,4},{4,8},{8,12},{12,16},{16,20},{20,24},{24,28},{1,5},{5,9},{9,... | collective-permute-start | bytes 405512 | tf_op jit(solution)/shard_map/while/body/eval_jaxpr/ppermute | solution.py:19
  288.9 75.2 %conditional.4 = ((f32[640,256]{1,0:T(8,128)S(1)}, f32[4,3,128]{2,1,0:T(4,128)S(1)}, f32[4,3]{1,0:T(4,128)S(1)})) conditional(s32[]{:T(128)} %convert_element_type.24, (f32[640,256]{1,0:T(8,128)S(1)}, f32[4,3,128]{2,1,0:T(4,128)S(1)}, f32[4,3]{1,0:T(4,128)S(1)}) %tuple.183, (s32[]{:T(128)}, s32[]{:T(128)}, pred[]{:T(512)}, s32[]{:T(128)}, s32[]{:T(128)}, ...), branch_computations={%region_1.1_spmd, %region_2.11_spmd} | conditional | flops 903485 | bytes 12145628 | solution.py:146
  289.0 75.1 %while.54 = (s32[]{:T(128)}, f32[640,256]{1,0:T(8,128)S(1)}, f32[3,128]{1,0:T(4,128)S(1)}, f32[3]{0:T(128)S(1)}, s32[]{:T(128)}, /*index=5*/s32[]{:T(128)}, s32[]{:T(128)}, s32[]{:T(128)}) while((s32[]{:T(128)}, f32[640,256]{1,0:T(8,128)S(1)}, f32[3,128]{1,0:T(4,128)S(1)}, f32[3]{0:T(128)S(1)}, s32[]{:T(128)}, /*index=5*/s32[]{:T(128)}, ...), condition=%wide.region_11.10_spmd, body=%wide.region_3.0_spmd.sunk | while | flops 903471 | bytes 12139696 | solution.py:127
  289.0 25.2 %conditional.5 = ((f32[640,256]{1,0:T(8,128)S(1)}, f32[3,128]{1,0:T(4,128)S(1)}, f32[3]{0:T(128)S(1)})) conditional(s32[]{:T(128)} %convert_element_type.25, (f32[640,256]{1,0:T(8,128)S(1)}, f32[3,128]{1,0:T(4,128)S(1)}, f32[3]{0:T(128)S(1)}) %tuple.186, (s32[]{:T(128)}, s32[]{:T(128)}, f32[640,256]{1,0:T(8,128)S(1)}, s32[]{:T(128)}, ...), branch_computations={%region_4.2_spmd, %region_5.8_spmd} | conditional | flops 903467 | bytes 12139525 | solution.py:123
  304.4 4.4 scatter.26
  314.2 25.2 %conditional.5 = ((f32[640,256]{1,0:T(8,128)S(1)}, f32[3,128]{1,0:T(4,128)S(1)}, f32[3]{0:T(128)S(1)})) conditional(s32[]{:T(128)} %convert_element_type.25, (f32[640,256]{1,0:T(8,128)S(1)}, f32[3,128]{1,0:T(4,128)S(1)}, f32[3]{0:T(128)S(1)}) %tuple.186, (s32[]{:T(128)}, s32[]{:T(128)}, f32[640,256]{1,0:T(8,128)S(1)}, s32[]{:T(128)}, ...), branch_computations={%region_4.2_spmd, %region_5.8_spmd} | conditional | flops 903467 | bytes 12139525 | solution.py:123
  329.6 4.4 scatter.26
  339.3 24.8 %conditional.5 = ((f32[640,256]{1,0:T(8,128)S(1)}, f32[3,128]{1,0:T(4,128)S(1)}, f32[3]{0:T(128)S(1)})) conditional(s32[]{:T(128)} %convert_element_type.25, (f32[640,256]{1,0:T(8,128)S(1)}, f32[3,128]{1,0:T(4,128)S(1)}, f32[3]{0:T(128)S(1)}) %tuple.186, (s32[]{:T(128)}, s32[]{:T(128)}, f32[640,256]{1,0:T(8,128)S(1)}, s32[]{:T(128)}, ...), branch_computations={%region_4.2_spmd, %region_5.8_spmd} | conditional | flops 903467 | bytes 12139525 | solution.py:123
  354.7 4.4 scatter.26
  376.3 77.0 %collective-permute-start = (f32[132,256]{1,0:T(8,128)S(1)}, f32[132,256]{1,0:T(8,128)S(1)}, u32[]{:S(2)}, u32[]{:S(2)}) collective-permute-start(f32[132,256]{1,0:T(8,128)S(1)} %slice.505), channel_id=1, source_target_pairs={{0,4},{4,8},{8,12},{12,16},{16,20},{20,24},{24,28},{1,5},{5,9},{9,... | collective-permute-start | bytes 405512 | tf_op jit(solution)/shard_map/while/body/eval_jaxpr/ppermute | solution.py:19
  463.5 75.2 %conditional.4 = ((f32[640,256]{1,0:T(8,128)S(1)}, f32[4,3,128]{2,1,0:T(4,128)S(1)}, f32[4,3]{1,0:T(4,128)S(1)})) conditional(s32[]{:T(128)} %convert_element_type.24, (f32[640,256]{1,0:T(8,128)S(1)}, f32[4,3,128]{2,1,0:T(4,128)S(1)}, f32[4,3]{1,0:T(4,128)S(1)}) %tuple.183, (s32[]{:T(128)}, s32[]{:T(128)}, pred[]{:T(512)}, s32[]{:T(128)}, s32[]{:T(128)}, ...), branch_computations={%region_1.1_spmd, %region_2.11_spmd} | conditional | flops 903485 | bytes 12145628 | solution.py:146
  463.5 75.1 %while.54 = (s32[]{:T(128)}, f32[640,256]{1,0:T(8,128)S(1)}, f32[3,128]{1,0:T(4,128)S(1)}, f32[3]{0:T(128)S(1)}, s32[]{:T(128)}, /*index=5*/s32[]{:T(128)}, s32[]{:T(128)}, s32[]{:T(128)}) while((s32[]{:T(128)}, f32[640,256]{1,0:T(8,128)S(1)}, f32[3,128]{1,0:T(4,128)S(1)}, f32[3]{0:T(128)S(1)}, s32[]{:T(128)}, /*index=5*/s32[]{:T(128)}, ...), condition=%wide.region_11.10_spmd, body=%wide.region_3.0_spmd.sunk | while | flops 903471 | bytes 12139696 | solution.py:127
  463.6 25.2 %conditional.5 = ((f32[640,256]{1,0:T(8,128)S(1)}, f32[3,128]{1,0:T(4,128)S(1)}, f32[3]{0:T(128)S(1)})) conditional(s32[]{:T(128)} %convert_element_type.25, (f32[640,256]{1,0:T(8,128)S(1)}, f32[3,128]{1,0:T(4,128)S(1)}, f32[3]{0:T(128)S(1)}) %tuple.186, (s32[]{:T(128)}, s32[]{:T(128)}, f32[640,256]{1,0:T(8,128)S(1)}, s32[]{:T(128)}, ...), branch_computations={%region_4.2_spmd, %region_5.8_spmd} | conditional | flops 903467 | bytes 12139525 | solution.py:123
  479.0 4.4 scatter.26
  488.8 25.2 %conditional.5 = ((f32[640,256]{1,0:T(8,128)S(1)}, f32[3,128]{1,0:T(4,128)S(1)}, f32[3]{0:T(128)S(1)})) conditional(s32[]{:T(128)} %convert_element_type.25, (f32[640,256]{1,0:T(8,128)S(1)}, f32[3,128]{1,0:T(4,128)S(1)}, f32[3]{0:T(128)S(1)}) %tuple.186, (s32[]{:T(128)}, s32[]{:T(128)}, f32[640,256]{1,0:T(8,128)S(1)}, s32[]{:T(128)}, ...), branch_computations={%region_4.2_spmd, %region_5.8_spmd} | conditional | flops 903467 | bytes 12139525 | solution.py:123
  504.2 4.4 scatter.26
  513.9 24.8 %conditional.5 = ((f32[640,256]{1,0:T(8,128)S(1)}, f32[3,128]{1,0:T(4,128)S(1)}, f32[3]{0:T(128)S(1)})) conditional(s32[]{:T(128)} %convert_element_type.25, (f32[640,256]{1,0:T(8,128)S(1)}, f32[3,128]{1,0:T(4,128)S(1)}, f32[3]{0:T(128)S(1)}) %tuple.186, (s32[]{:T(128)}, s32[]{:T(128)}, f32[640,256]{1,0:T(8,128)S(1)}, s32[]{:T(128)}, ...), branch_computations={%region_4.2_spmd, %region_5.8_spmd} | conditional | flops 903467 | bytes 12139525 | solution.py:123
  529.3 4.4 scatter.26
  550.9 77.0 %collective-permute-start = (f32[132,256]{1,0:T(8,128)S(1)}, f32[132,256]{1,0:T(8,128)S(1)}, u32[]{:S(2)}, u32[]{:S(2)}) collective-permute-start(f32[132,256]{1,0:T(8,128)S(1)} %slice.505), channel_id=1, source_target_pairs={{0,4},{4,8},{8,12},{12,16},{16,20},{20,24},{24,28},{1,5},{5,9},{9,... | collective-permute-start | bytes 405512 | tf_op jit(solution)/shard_map/while/body/eval_jaxpr/ppermute | solution.py:19
  638.1 75.2 %conditional.4 = ((f32[640,256]{1,0:T(8,128)S(1)}, f32[4,3,128]{2,1,0:T(4,128)S(1)}, f32[4,3]{1,0:T(4,128)S(1)})) conditional(s32[]{:T(128)} %convert_element_type.24, (f32[640,256]{1,0:T(8,128)S(1)}, f32[4,3,128]{2,1,0:T(4,128)S(1)}, f32[4,3]{1,0:T(4,128)S(1)}) %tuple.183, (s32[]{:T(128)}, s32[]{:T(128)}, pred[]{:T(512)}, s32[]{:T(128)}, s32[]{:T(128)}, ...), branch_computations={%region_1.1_spmd, %region_2.11_spmd} | conditional | flops 903485 | bytes 12145628 | solution.py:146
  638.1 75.1 %while.54 = (s32[]{:T(128)}, f32[640,256]{1,0:T(8,128)S(1)}, f32[3,128]{1,0:T(4,128)S(1)}, f32[3]{0:T(128)S(1)}, s32[]{:T(128)}, /*index=5*/s32[]{:T(128)}, s32[]{:T(128)}, s32[]{:T(128)}) while((s32[]{:T(128)}, f32[640,256]{1,0:T(8,128)S(1)}, f32[3,128]{1,0:T(4,128)S(1)}, f32[3]{0:T(128)S(1)}, s32[]{:T(128)}, /*index=5*/s32[]{:T(128)}, ...), condition=%wide.region_11.10_spmd, body=%wide.region_3.0_spmd.sunk | while | flops 903471 | bytes 12139696 | solution.py:127
  638.2 25.2 %conditional.5 = ((f32[640,256]{1,0:T(8,128)S(1)}, f32[3,128]{1,0:T(4,128)S(1)}, f32[3]{0:T(128)S(1)})) conditional(s32[]{:T(128)} %convert_element_type.25, (f32[640,256]{1,0:T(8,128)S(1)}, f32[3,128]{1,0:T(4,128)S(1)}, f32[3]{0:T(128)S(1)}) %tuple.186, (s32[]{:T(128)}, s32[]{:T(128)}, f32[640,256]{1,0:T(8,128)S(1)}, s32[]{:T(128)}, ...), branch_computations={%region_4.2_spmd, %region_5.8_spmd} | conditional | flops 903467 | bytes 12139525 | solution.py:123
  653.6 4.4 scatter.26
  663.4 25.2 %conditional.5 = ((f32[640,256]{1,0:T(8,128)S(1)}, f32[3,128]{1,0:T(4,128)S(1)}, f32[3]{0:T(128)S(1)})) conditional(s32[]{:T(128)} %convert_element_type.25, (f32[640,256]{1,0:T(8,128)S(1)}, f32[3,128]{1,0:T(4,128)S(1)}, f32[3]{0:T(128)S(1)}) %tuple.186, (s32[]{:T(128)}, s32[]{:T(128)}, f32[640,256]{1,0:T(8,128)S(1)}, s32[]{:T(128)}, ...), branch_computations={%region_4.2_spmd, %region_5.8_spmd} | conditional | flops 903467 | bytes 12139525 | solution.py:123
  688.5 24.8 %conditional.5 = ((f32[640,256]{1,0:T(8,128)S(1)}, f32[3,128]{1,0:T(4,128)S(1)}, f32[3]{0:T(128)S(1)})) conditional(s32[]{:T(128)} %convert_element_type.25, (f32[640,256]{1,0:T(8,128)S(1)}, f32[3,128]{1,0:T(4,128)S(1)}, f32[3]{0:T(128)S(1)}) %tuple.186, (s32[]{:T(128)}, s32[]{:T(128)}, f32[640,256]{1,0:T(8,128)S(1)}, s32[]{:T(128)}, ...), branch_computations={%region_4.2_spmd, %region_5.8_spmd} | conditional | flops 903467 | bytes 12139525 | solution.py:123
  725.5 77.0 %collective-permute-start = (f32[132,256]{1,0:T(8,128)S(1)}, f32[132,256]{1,0:T(8,128)S(1)}, u32[]{:S(2)}, u32[]{:S(2)}) collective-permute-start(f32[132,256]{1,0:T(8,128)S(1)} %slice.505), channel_id=1, source_target_pairs={{0,4},{4,8},{8,12},{12,16},{16,20},{20,24},{24,28},{1,5},{5,9},{9,... | collective-permute-start | bytes 405512 | tf_op jit(solution)/shard_map/while/body/eval_jaxpr/ppermute | solution.py:19
  819.7 80.7 %collective-permute-done.1 = f32[132,256]{1,0:T(8,128)S(1)} collective-permute-done((f32[132,256]{1,0:T(8,128)S(1)}, f32[132,256]{1,0:T(8,128)S(1)}, u32[]{:S(2)}, u32[]{:S(2)}) %collective-permute-start.1) | collective-permute-done | bytes 135200 | tf_op jit(solution)/shard_map/while/body/eval_jaxpr/ppermute | solution.py:20
  908.5 4.9 collective-permute-done.1
  914.6 76.1 %collective-permute-start = (f32[132,256]{1,0:T(8,128)S(1)}, f32[132,256]{1,0:T(8,128)S(1)}, u32[]{:S(2)}, u32[]{:S(2)}) collective-permute-start(f32[132,256]{1,0:T(8,128)S(1)} %slice.505), channel_id=1, source_target_pairs={{0,4},{4,8},{8,12},{12,16},{16,20},{20,24},{24,28},{1,5},{5,9},{9,... | collective-permute-start | bytes 405512 | tf_op jit(solution)/shard_map/while/body/eval_jaxpr/ppermute | solution.py:19
  995.8 5.8 collective-permute-done.1
  1009.7 74.7 %collective-permute-done.1 = f32[132,256]{1,0:T(8,128)S(1)} collective-permute-done((f32[132,256]{1,0:T(8,128)S(1)}, f32[132,256]{1,0:T(8,128)S(1)}, u32[]{:S(2)}, u32[]{:S(2)}) %collective-permute-start.1) | collective-permute-done | bytes 135200 | tf_op jit(solution)/shard_map/while/body/eval_jaxpr/ppermute | solution.py:20
  1092.5 4.9 collective-permute-done.1
  1100.2 74.4 %collective-permute-start.3 = (f32[128,128]{1,0:T(8,128)S(1)}, f32[128,128]{1,0:T(8,128)S(1)}, u32[]{:S(2)}, u32[]{:S(2)}) collective-permute-start(f32[128,128]{1,0:T(8,128)S(1)} %slice.442), channel_id=1, source_target_pairs={{0,4},{4,8},{8,12},{12,16},{16,20},{20,24},{24,28},{1,5},{5,9},{9,... | collective-permute-start | bytes 196616 | tf_op jit(solution)/shard_map/ppermute | solution.py:28
  1177.9 6.7 collective-permute-done.4
  1192.6 24.5 %collective-permute-done.6 = f32[128,128]{1,0:T(8,128)S(1)} collective-permute-done((f32[128,128]{1,0:T(8,128)S(1)}, f32[128,128]{1,0:T(8,128)S(1)}, u32[]{:S(2)}, u32[]{:S(2)}) %collective-permute-start.6) | collective-permute-done | bytes 65568 | tf_op jit(solution)/shard_map/ppermute | solution.py:28
  1224.7 4.4 collective-permute-done.8
  (824 shorter events, 404.7 us)
Async XLA Ops:
  0.6 3.5 copy-start.3
  1.5 1097.1 %collective-permute-start.2 = (f32[128,128]{1,0:T(8,128)S(1)}, f32[128,128]{1,0:T(8,128)S(1)}, u32[]{:S(2)}, u32[]{:S(2)}) collective-permute-start(f32[128,128]{1,0:T(8,128)S(1)} %slice.403), channel_id=1, source_target_pairs={{4,0},{8,4},{12,8},{16,12},{20,16},{24,20},{28,24},{5,1},{9,5},{13... | collective-permute-start | bytes 196616 | tf_op jit(solution)/shard_map/ppermute | solution.py:28
  17.7 1080.9 %copy-start.1 = (f32[384,128]{1,0:T(8,128)S(1)}, f32[384,128]{1,0:T(8,128)}, u32[]{:S(2)}) copy-start(f32[384,128]{1,0:T(8,128)} %param.39) | copy-start | bytes 589828
  17.8 7.3 collective-permute-start
  25.1 7.1 collective-permute-start.1
  33.3 73.5 %collective-permute-start = (f32[132,256]{1,0:T(8,128)S(1)}, f32[132,256]{1,0:T(8,128)S(1)}, u32[]{:S(2)}, u32[]{:S(2)}) collective-permute-start(f32[132,256]{1,0:T(8,128)S(1)} %slice.505), channel_id=1, source_target_pairs={{0,4},{4,8},{8,12},{12,16},{16,20},{20,24},{24,28},{1,5},{5,9},{9,... | collective-permute-start | bytes 405512 | tf_op jit(solution)/shard_map/while/body/eval_jaxpr/ppermute | solution.py:19
  106.9 6.4 collective-permute-start.1
  123.4 0.7 copy-start.2
  127.7 0.7 copy-start.4
  148.6 0.7 copy-start.2
  189.6 3.9 collective-permute-start
  193.5 7.1 collective-permute-start.1
  201.7 79.0 %collective-permute-start = (f32[132,256]{1,0:T(8,128)S(1)}, f32[132,256]{1,0:T(8,128)S(1)}, u32[]{:S(2)}, u32[]{:S(2)}) collective-permute-start(f32[132,256]{1,0:T(8,128)S(1)} %slice.505), channel_id=1, source_target_pairs={{0,4},{4,8},{8,12},{12,16},{16,20},{20,24},{24,28},{1,5},{5,9},{9,... | collective-permute-start | bytes 405512 | tf_op jit(solution)/shard_map/while/body/eval_jaxpr/ppermute | solution.py:19
  280.7 7.1 collective-permute-start.1
  364.2 3.9 collective-permute-start
  368.1 7.1 collective-permute-start.1
  376.3 79.0 %collective-permute-start = (f32[132,256]{1,0:T(8,128)S(1)}, f32[132,256]{1,0:T(8,128)S(1)}, u32[]{:S(2)}, u32[]{:S(2)}) collective-permute-start(f32[132,256]{1,0:T(8,128)S(1)} %slice.505), channel_id=1, source_target_pairs={{0,4},{4,8},{8,12},{12,16},{16,20},{20,24},{24,28},{1,5},{5,9},{9,... | collective-permute-start | bytes 405512 | tf_op jit(solution)/shard_map/while/body/eval_jaxpr/ppermute | solution.py:19
  455.3 7.1 collective-permute-start.1
  472.6 0.7 copy-start.2
  538.8 3.9 collective-permute-start
  542.7 7.1 collective-permute-start.1
  550.9 79.0 %collective-permute-start = (f32[132,256]{1,0:T(8,128)S(1)}, f32[132,256]{1,0:T(8,128)S(1)}, u32[]{:S(2)}, u32[]{:S(2)}) collective-permute-start(f32[132,256]{1,0:T(8,128)S(1)} %slice.505), channel_id=1, source_target_pairs={{0,4},{4,8},{8,12},{12,16},{16,20},{20,24},{24,28},{1,5},{5,9},{9,... | collective-permute-start | bytes 405512 | tf_op jit(solution)/shard_map/while/body/eval_jaxpr/ppermute | solution.py:19
  629.9 7.1 collective-permute-start.1
  647.2 0.7 copy-start.2
  672.4 0.7 copy-start.2
  713.3 3.9 collective-permute-start
  717.3 7.1 collective-permute-start.1
  725.5 79.0 %collective-permute-start = (f32[132,256]{1,0:T(8,128)S(1)}, f32[132,256]{1,0:T(8,128)S(1)}, u32[]{:S(2)}, u32[]{:S(2)}) collective-permute-start(f32[132,256]{1,0:T(8,128)S(1)} %slice.505), channel_id=1, source_target_pairs={{0,4},{4,8},{8,12},{12,16},{16,20},{20,24},{24,28},{1,5},{5,9},{9,... | collective-permute-start | bytes 405512 | tf_op jit(solution)/shard_map/while/body/eval_jaxpr/ppermute | solution.py:19
  804.5 7.1 collective-permute-start.1
  812.7 3.9 collective-permute-start
  816.7 83.7 %collective-permute-start.1 = (f32[132,256]{1,0:T(8,128)S(1)}, f32[132,256]{1,0:T(8,128)S(1)}, u32[]{:S(2)}, u32[]{:S(2)}) collective-permute-start(f32[132,256]{1,0:T(8,128)S(1)} %get-tuple-element.847), channel_id=1, source_target_pairs={{4,0},{8,4},{12,8},{16,12},{20,16},{24,20},{28,24},{5,1},{9,5},{13... | collective-permute-start | bytes 405512 | tf_op jit(solution)/shard_map/while/body/eval_jaxpr/ppermute | solution.py:20
  901.5 3.9 collective-permute-start
  905.5 8.0 collective-permute-start.1
  914.6 78.1 %collective-permute-start = (f32[132,256]{1,0:T(8,128)S(1)}, f32[132,256]{1,0:T(8,128)S(1)}, u32[]{:S(2)}, u32[]{:S(2)}) collective-permute-start(f32[132,256]{1,0:T(8,128)S(1)} %slice.505), channel_id=1, source_target_pairs={{0,4},{4,8},{8,12},{12,16},{16,20},{20,24},{24,28},{1,5},{5,9},{9,... | collective-permute-start | bytes 405512 | tf_op jit(solution)/shard_map/while/body/eval_jaxpr/ppermute | solution.py:19
  992.7 8.9 collective-permute-start.1
  1002.7 3.9 collective-permute-start
  1006.7 77.7 %collective-permute-start.1 = (f32[132,256]{1,0:T(8,128)S(1)}, f32[132,256]{1,0:T(8,128)S(1)}, u32[]{:S(2)}, u32[]{:S(2)}) collective-permute-start(f32[132,256]{1,0:T(8,128)S(1)} %get-tuple-element.847), channel_id=1, source_target_pairs={{4,0},{8,4},{12,8},{16,12},{20,16},{24,20},{28,24},{5,1},{9,5},{13... | collective-permute-start | bytes 405512 | tf_op jit(solution)/shard_map/while/body/eval_jaxpr/ppermute | solution.py:20
  1085.5 3.9 collective-permute-start
  1089.5 8.0 collective-permute-start.1
  1100.2 75.7 %collective-permute-start.3 = (f32[128,128]{1,0:T(8,128)S(1)}, f32[128,128]{1,0:T(8,128)S(1)}, u32[]{:S(2)}, u32[]{:S(2)}) collective-permute-start(f32[128,128]{1,0:T(8,128)S(1)} %slice.442), channel_id=1, source_target_pairs={{0,4},{4,8},{8,12},{12,16},{16,20},{20,24},{24,28},{1,5},{5,9},{9,... | collective-permute-start | bytes 196616 | tf_op jit(solution)/shard_map/ppermute | solution.py:28
  1176.0 8.7 collective-permute-start.4
  1186.2 3.2 collective-permute-start.5
  1189.5 27.6 %collective-permute-start.6 = (f32[128,128]{1,0:T(8,128)S(1)}, f32[128,128]{1,0:T(8,128)S(1)}, u32[]{:S(2)}, u32[]{:S(2)}) collective-permute-start(f32[128,128]{1,0:T(8,128)S(1)} %slice_select_fusion.4), channel_id=1, source_target_pairs={{4,0},{8,4},{12,8},{16,12},{20,16},{24,20},{28,24},{5,1},{9,5},{13... | collective-permute-start | bytes 196616 | tf_op jit(solution)/shard_map/ppermute | solution.py:28
  1191.7 0.8 copy-start
  1217.6 6.4 slice-start
  1218.7 3.2 collective-permute-start.7
  1222.0 7.1 collective-permute-start.8
  1230.6 3.2 collective-permute-start.9
  (18 other events, 11.9 us)
where the time goes:
time: 1240 us; the launch traced here: 1230 us
  starting transfers between devices  524 us (42%)
  waiting for transfers between devices  351 us (28%)
  local copies, waits for them, and re-layouts  225 us (18%)
  other arithmetic  72.4 us (6%)
  loops' own time  30.1 us (2%)
  matrix products  17.5 us (1%)
  blocking collectives  13.4 us (1%)
    ppermute x15, starting transfers between devices, padded_2(): before = lax.ppermute(last, axis, up)  407 us
    ppermute x15, waiting for transfers between devices, padded_2(): after = lax.ppermute(first, axis, down)  211 us
    ppermute x15, waiting for transfers between devices, padded_2(): before = lax.ppermute(last, axis, up)  99.1 us
    ppermute x8, starting transfers between devices, from_behind(): return lax.ppermute(x, axis, pairs)  88.6 us
    scatter x12, local copies, waits for them, and re-layouts, chase_step(): dense_rows.at[:half_width, offset:offset + double]  52.2 us
    another operation x72, other arithmetic  41.1 us
    ppermute x8, waiting for transfers between devices, from_behind(): return lax.ppermute(x, axis, pairs)  40.9 us
    another operation x57, local copies, waits for them, and re-layouts  32.4 us
  transfers between devices with their start and end apart: 38, of which 37 were waited for; matrix products, arithmetic and copies ran while one was open for 24% of the time, Pallas kernels for 0%

commit v1 on v0

v1 whole, which is shorter than its diff:
```python
import functools

import jax
import jax.numpy as jnp
from jax import lax
from jax.experimental import pallas as pl
from jax.experimental.pallas import tpu as pltpu
from jax.sharding import PartitionSpec as P

SWEEPS = 4
LAG = 3


def chase_kernel(blocks, half, blocks_dev, halo, piece_count, sweeps, *refs):
    band_ref, eig_ref, band_out, eig_out = refs[:4]
    d_refs = refs[4 : 5 + sweeps]
    l_refs = refs[5 + sweeps : 6 + 2 * sweeps]
    v_refs = refs[6 + 2 * sweeps : 6 + 3 * sweeps]
    tau_refs = refs[6 + 3 * sweeps : 6 + 4 * sweeps]
    x_refs = refs[6 + 4 * sweeps : 6 + 5 * sweeps]
    edge_ref, rest_ref, turn_ref = refs[6 + 5 * sweeps :]
    steps = blocks - 2
    row = lax.broadcasted_iota(jnp.int32, (half, half), 0)
    col = lax.broadcasted_iota(jnp.int32, (half, half), 1)
    lane = lax.broadcasted_iota(jnp.int32, (1, half), 1)
    eye = row == col
    row8 = lax.broadcasted_iota(jnp.int32, (8, half), 0)
    col8 = lax.broadcasted_iota(jnp.int32, (8, half), 1)
    zero = jnp.zeros((half, half), jnp.float32)

    def slot(k):
        return jnp.clip(k, -1, blocks + 1) + 1

    def unpack(block):
        dev = block // blocks_dev
        part = block % blocks_dev
        start = pl.multiple_of(part * half, half)
        piece = band_ref[dev, :half, pl.ds(start, half)]
        extra = band_ref[dev, half : half + 1, pl.ds(start, half)]
        rows = pltpu.roll(piece.T, 0, 1, stride=1, stride_axis=0)
        d_refs[0][slot(block)] = jnp.where(row >= col, rows, rows.T)
        l_refs[0][slot(block - 1)] = jnp.where(
            col > row, rows, jnp.where(eye, jnp.broadcast_to(extra, (half, half)), 0.0)
        )

    def unpack_step(block, carry):
        unpack(block)
        return carry

    lax.fori_loop(0, blocks, unpack_step, 0)
    for extra_block in (blocks, blocks + 1):
        d_refs[0][extra_block + 1] = zero
    for extra_block in (blocks - 1, blocks, blocks + 1):
        l_refs[0][extra_block + 1] = zero
    edge_ref[...] = jnp.zeros(edge_ref.shape, jnp.float32)
    rest_ref[...] = zero

    def chain(s, t):
        k = t - LAG * s
        here, after, before = slot(k), slot(k + 1), slot(k - 1)
        old, new = s, s + 1
        d_prev, l_prev, d_now, l_now = d_refs[s], l_refs[s], d_refs[s + 1], l_refs[s + 1]
        active = (k >= 0) & (k < steps)
        limit = jnp.where(active, half, 0)
        pick = jnp.where(active, new, -1)
        x = x_refs[s][...]
        d_old, l_old, d_next = d_prev[here], l_prev[here], d_prev[after]
        l_next = l_prev[after, old : old + 1, :]
        left = l_now[before]

        lead = jnp.where(lane == old, d_next[old : old + 1, :], l_old[old : old + 1, :])
        lead_col = jnp.sum(
            jnp.where(eye, jnp.broadcast_to(lead, (half, half)), 0.0), axis=1, keepdims=True
        )
        window = jnp.where(row == old, lead, jnp.where(col == old, lead_col, d_old))
        rest_row = rest_ref[old : old + 1, :]
        feed = jnp.where(k == steps - 2, half, 0)
        corner = jnp.where(lane == old, l_next, jnp.where(lane < feed, rest_row, 0.0))
        if s > 0:
            rest_ref[...] = jnp.where(
                col == jnp.where(k == steps - 1, old, -1), l_old, rest_ref[...]
            )
        below = jnp.where(row == old, corner, jnp.where(col == old, d_next, l_old))

        rest = jnp.sum(jnp.where(row == new, 0.0, x * x), axis=0, keepdims=True)
        top = x[new : new + 1, :]
        length = jnp.sqrt(rest + top * top)
        v_top = top + length
        tau = 2.0 / (rest + v_top * v_top)
        tau = jnp.where(lane < limit, tau, 0.0)
        v_col = jnp.where(row < limit, jnp.where(row == new, v_top, x), 0.0)
        v_row = jnp.sum(jnp.where(eye, v_col, 0.0), axis=0, keepdims=True)

        beneath = jnp.sum(below * v_row, axis=1, keepdims=True)
        beneath = jnp.where(row < limit, beneath * tau, 0.0)
        first = k < 0
        source = jnp.where(first, old, new)
        head = jnp.where(row == old, l_next, d_next)
        early = jnp.where(first, half, 0)
        column = jnp.where(row < early, head, below)
        column = jnp.sum(jnp.where(col == source, column, 0.0), axis=1, keepdims=True)
        x_refs[s][...] = column - jnp.where(row < limit, beneath * v_top, 0.0)
        below = below - beneath * v_row

        inside = tau * jnp.sum(v_col * window, axis=0, keepdims=True)
        scale = 0.5 * tau * jnp.sum(v_row * inside, axis=1, keepdims=True)
        z_row = inside - scale * v_row
        z_col = jnp.sum(
            jnp.where(eye, jnp.broadcast_to(z_row, (half, half)), 0.0), axis=1, keepdims=True
        )
        window = window - v_col * z_row - z_col * v_row

        across = tau * jnp.sum(v_col * left, axis=0, keepdims=True)
        left = left - v_col * across
        left = jnp.where(col == pick, jnp.where(row == new, -length, 0.0), left)

        l_now[before] = left
        d_now[here] = window
        l_now[here] = below
        v_refs[s][here] = v_col
        tau_refs[s][here] = jnp.broadcast_to(tau, (8, half))

        start = jnp.where(k == 0, s, -1)
        edge = edge_ref[...]
        edge = jnp.where((row8 == start) & (col8 == s), d_old[:8], edge)
        below_start = jnp.where(k == 0, s + 1, -1)
        edge = jnp.where((row8 == below_start) & (col8 == s), -length, edge)
        edge_ref[...] = edge

    def wave(t, carry):
        for s in reversed(range(sweeps)):
            chain(s, t)
        return carry

    lax.fori_loop(-1, blocks + LAG * (sweeps - 1), wave, 0)

    device = lax.axis_index("band")
    base = device * blocks_dev - halo
    eig = [eig_ref[e * half : (e + 1) * half, :] for e in range(halo + blocks_dev)]
    eig.append(eig_ref[(halo + blocks_dev) * half : (halo + blocks_dev) * half + 8, :])
    for s in reversed(range(sweeps)):
        lead_rows = s + 1
        for e in range(sweeps - 1 - s + halo - sweeps, halo + blocks_dev):
            k = base + e
            v = v_refs[s][slot(k)]
            tau = tau_refs[s][slot(k), 0:1, :]
            low, high = eig[e], eig[e + 1]
            mixed = jnp.concatenate([jnp.where(row8 < lead_rows, high[:8], low[:8]), low[8:]], 0)
            inner = tau * jnp.sum(v * mixed, axis=0, keepdims=True)
            mixed = mixed - v * inner
            eig[e] = jnp.concatenate([jnp.where(row8 < lead_rows, low[:8], mixed[:8]), mixed[8:]], 0)
            top = jnp.where(row8 < lead_rows, mixed[:8], high[:8])
            eig[e + 1] = jnp.concatenate([top, high[8:]], 0) if high.shape[0] > 8 else top
    for m in range(blocks_dev):
        eig_out[m * half : (m + 1) * half, :] = eig[halo + m]

    d_last, l_last = d_refs[sweeps], l_refs[sweeps]
    edge = jnp.concatenate([edge_ref[...], zero[8:]], axis=0)
    rest = rest_ref[...]
    d_last[0] = jnp.where(row < sweeps, edge, 0.0)
    l_last[0] = jnp.where(row >= sweeps, edge, 0.0)
    flip = jnp.where((row + col == half) | ((row == 0) & (col == 0)), 1.0, 0.0)
    position = lax.axis_index("cols") * piece_count
    for m in range(blocks_dev):
        b = device * blocks_dev + m
        lim = jnp.where(b > 0, half, 0)
        rest_below = jnp.where(b == steps, half, 0)
        rest_last = jnp.where(b == steps + 1, half, 0)
        d_here, d_before = d_last[slot(b)], d_last[slot(b - 1)]
        l_here, l_before = l_last[slot(b - 1)], l_last[slot(b - 2)]
        c0 = jnp.where(
            row >= sweeps, jnp.where(col >= sweeps, d_here, l_here), jnp.where(col < sweeps, d_before, 0.0)
        )
        c1 = jnp.where(
            row >= sweeps,
            jnp.where(col >= sweeps, l_here, jnp.where(row < rest_below, rest, 0.0)),
            jnp.where(col >= sweeps, d_before, l_before),
        )
        c1 = jnp.where(row < lim, c1, 0.0)
        c2 = jnp.where(col >= sweeps, l_before, jnp.where(row < rest_last, rest, 0.0))
        c2 = jnp.where(row < sweeps, c2, 0.0)
        c2 = jnp.where(row < lim, c2, 0.0)
        lower = jnp.where(col <= row, c0, c1)
        upper = jnp.where(col <= row, c1, c2)
        for n, part in enumerate((lower, upper)):
            turned = jnp.dot(part, flip, precision=lax.Precision.HIGHEST)
            turned = pltpu.roll(turned, 0, 1, stride=1, stride_axis=0)
            turn_ref[n * half : (n + 1) * half, :] = turned.T
        band_out[:, m * half : (m + 1) * half] = turn_ref[pl.ds(pl.multiple_of(position, 8), piece_count), :]


def shifted(x, axis, by):
    peers = lax.axis_size(axis)
    pairs = [(i, i + by) for i in range(peers) if 0 <= i + by < peers]
    return lax.ppermute(x, axis, pairs)


def body(band_diagonals, eigenvectors):
    piece_count, rows_dev = band_diagonals.shape
    double = piece_count * lax.axis_size("cols")
    half = double // 2
    blocks_dev = rows_dev // half
    devices = lax.axis_size("band")
    blocks = blocks_dev * devices
    sweeps = SWEEPS
    pieces = lax.all_gather(band_diagonals, "cols", axis=0, tiled=True)
    turned = jnp.concatenate(
        [pieces[:1], pieces[half - 1 : 0 : -1], pieces[half : half + 8]], axis=0
    )
    band = lax.all_gather(turned, "band", axis=0, tiled=False)

    halo = sweeps
    parts = []
    need = halo * half
    hop = 1
    while need > 0:
        take = min(need, rows_dev)
        parts.insert(0, shifted(eigenvectors[rows_dev - take :], "band", hop))
        need -= take
        hop += 1
    parts.append(eigenvectors)
    parts.append(shifted(eigenvectors[:8], "band", -1))
    eig = jnp.concatenate(parts, axis=0)
    columns = eigenvectors.shape[1]

    slots = blocks + 3
    f32 = jnp.float32
    scratch = (
        [pltpu.VMEM((slots, half, half), f32)] * (2 * (sweeps + 1))
        + [pltpu.VMEM((slots, half, half), f32)] * sweeps
        + [pltpu.VMEM((slots, 8, half), f32)] * sweeps
        + [pltpu.VMEM((half, half), f32)] * sweeps
        + [
            pltpu.VMEM((8, half), f32),
            pltpu.VMEM((half, half), f32),
            pltpu.VMEM((double, half), f32),
        ]
    )
    vmem = pl.BlockSpec(memory_space=pltpu.VMEM)
    return pl.pallas_call(
        functools.partial(chase_kernel, blocks, half, blocks_dev, halo, piece_count, sweeps),
        out_shape=(
            jax.ShapeDtypeStruct((piece_count, rows_dev), f32),
            jax.ShapeDtypeStruct((rows_dev, columns), f32),
        ),
        in_specs=[vmem, vmem],
        out_specs=(vmem, vmem),
        scratch_shapes=scratch,
        compiler_params=pltpu.CompilerParams(vmem_limit_bytes=62 * 1024 * 1024),
    )(band, eig)


def solution(mesh):
    return jax.shard_map(
        body,
        mesh=mesh,
        in_specs=(P("cols", "band"), P("band", "cols")),
        out_specs=(P("cols", "band"), P("band", "cols")),
        check_vma=False,
    )
```

time: 1240 us -> 86.7 us (0.07)
  starting transfers between devices: 524 us -> 12.4 us
  waiting for transfers between devices: 351 us -> 18 us
  local copies, waits for them, and re-layouts: 225 us -> 0.18 us
  other arithmetic: 72.4 us -> 1.5 us
  loops' own time: 30.1 us -> 0 us
  Pallas kernels: 0 us -> 26.9 us
  matrix products: 17.5 us -> 0 us
  between operations: 1.08 us -> 14.1 us
    ppermute x38 -> x3, starting transfers between devices: 524 us -> 12.3 us  [shifted(): return lax.ppermute(x, axis, pairs)]
    ppermute x38 -> x3, waiting for transfers between devices: 351 us -> 3.41 us  [shifted(): return lax.ppermute(x, axis, pairs)]
    scatter x106 -> x0, local copies, waits for them, and re-layouts: 107 us -> none  [the longest x12 52.2 us: chase_step(): dense_rows.at[:half_width, offset:offset + double]]
    another operation x72 -> x0, other arithmetic: 41.1 us -> none
    another operation x57 -> x0, local copies, waits for them, and re-layouts: 32.4 us -> none
    another operation x32 -> x0, loops' own time: 30.1 us -> none  [the longest x12 27.1 us: advance(): return lax.cond(step_index < local_steps, apply_step, keep_same, carry)]
    pallas_call x0 -> x1, Pallas kernels: none -> 26.9 us  [body(): pl.pallas_call(functools.partial(chase_kernel, blocks, half, blocks_dev,...]
    cond x144 -> x0, local copies, waits for them, and re-layouts: 23.5 us -> none
  transfers between devices with their start and end apart: 38 -> 4, of which waited for: 37 -> 2; matrix products, arithmetic and copies ran while one was open for 24% -> 1% of each run, Pallas kernels for 0% -> 0%
where the time goes in v1:
time: 86.7 us; the launch traced here: 85.1 us
  Pallas kernels  26.9 us (31%)
  waiting for transfers between devices  18 us (21%)
  between operations  14.1 us (16%)
  starting transfers between devices  12.4 us (14%)
  blocking collectives  12 us (14%)
  other arithmetic  1.5 us (2%)
    pallas_call x1, Pallas kernels, body(): pl.pallas_call(functools.partial(chase_kernel, blocks, half, blocks_dev,...  26.9 us
    all_gather x1, waiting for transfers between devices, body(): band = lax.all_gather(turned, 'band', axis=0, tiled=False)  14.6 us
    ppermute x3, starting transfers between devices, shifted(): return lax.ppermute(x, axis, pairs)  12.3 us
    all_gather x1, blocking collectives, body(): pieces = lax.all_gather(band_diagonals, 'cols', axis=0, tiled=True)  12 us
    ppermute x3, waiting for transfers between devices, shifted(): return lax.ppermute(x, axis, pairs)  3.41 us
  transfers between devices with their start and end apart: 4, of which 2 were waited for; matrix products, arithmetic and copies ran while one was open for 1% of the time, Pallas kernels for 0%

profile of v1, /device:TPU:25, one launch (start us, length us, event | category | flops | bytes accessed | tf_op | source)
XLA Modules:
  0.0 85.1 jit_solution(6566526971252606629)
XLA Ops:
  7.2 0.0 copy-start
  7.2 0.0 all-gather.3.cloned.1.call-start
  7.2 12.0 %all_gather.9 = f32[256,384]{1,0:T(8,128)S(1)} all-gather(f32[64,384]{1,0:T(8,128)} %param.2), channel_id=1, replica_groups=mesh['band'=8,'cols'=4] {'cols'}, dimensions={0}, use_global_device_ids=true | all-gather | bytes 491520 | tf_op jit(solution)/shard_map/all_gather | solution.py:206
  19.3 0.1 rev.3
  19.4 0.7 pad_maximum_fusion.1
  20.1 0.0 all-gather.3.cloned.1.call-update
  20.1 0.0 copy-done
  20.1 7.3 %collective-permute-start.1 = (f32[384,128]{1,0:T(8,128)S(1)}, f32[384,128]{1,0:T(8,128)S(1)}, u32[]{:S(2)}, u32[]{:S(2)}) collective-permute-start(f32[384,128]{1,0:T(8,128)S(1)} %copy-done), channel_id=1, source_target_pairs={{0,4},{4,8},{8,12},{12,16},{16,20},{20,24},{24,28},{1,5},{5,9},{9,... | collective-permute-start | bytes 589832 | tf_op jit(solution)/shard_map/ppermute | solution.py:195
  27.5 3.1 %collective-permute-start = (f32[128,128]{1,0:T(8,128)S(1)}, f32[128,128]{1,0:T(8,128)S(1)}, u32[]{:S(2)}, u32[]{:S(2)}) collective-permute-start(f32[128,128]{1,0:T(8,128)S(1)} %slice.18), channel_id=1, source_target_pairs={{0,8},{4,12},{8,16},{12,20},{16,24},{20,28},{1,9},{5,13},{9,17},{1... | collective-permute-start | bytes 196616 | tf_op jit(solution)/shard_map/ppermute | solution.py:195
  30.6 1.9 %collective-permute-start.2 = (f32[8,128]{1,0:T(8,128)S(1)}, f32[8,128]{1,0:T(8,128)S(1)}, u32[]{:S(2)}, u32[]{:S(2)}) collective-permute-start(f32[8,128]{1,0:T(8,128)S(1)} %slice.19), channel_id=1, source_target_pairs={{4,0},{8,4},{12,8},{16,12},{20,16},{24,20},{28,24},{5,1},{9,5},{13... | collective-permute-start | bytes 12296 | tf_op jit(solution)/shard_map/ppermute | solution.py:195
  32.5 3.4 %collective-permute-done.2 = f32[8,128]{1,0:T(8,128)S(1)} collective-permute-done((f32[8,128]{1,0:T(8,128)S(1)}, f32[8,128]{1,0:T(8,128)S(1)}, u32[]{:S(2)}, u32[]{:S(2)}) %collective-permute-start.2) | collective-permute-done | bytes 4128 | tf_op jit(solution)/shard_map/ppermute | solution.py:195
  35.9 0.0 collective-permute-done
  35.9 0.0 collective-permute-done.1
  35.9 0.8 pad_maximum_fusion.refs_1_
  36.7 14.6 %all-gather.3.cloned.1.call-done = f32[1088,384]{1,0:T(8,128)} async-done(((f32[136,384]{1,0:T(8,128)}), f32[1088,384]{1,0:T(8,128)}) %all-gather.3.cloned.1.call-update) | async-done | bytes 1671184 | tf_op jit(solution)/shard_map/all_gather | solution.py:210
  51.3 26.9 %shard_map.41 = (f32[64,384]{1,0:T(8,128)}, f32[384,128]{1,0:T(8,128)}) custom-call(f32[8,136,384]{2,1,0:T(8,128)} %bitcast.1, f32[904,128]{1,0:T(8,128)} %pad_maximum_fusion.refs_1_), custom_call_target="tpu_custom_call" | custom-call | tf_op jit(solution)/shard_map/pallas_call | solution.py:240
  (5 shorter events, 0.0 us)
Async XLA Ops:
  7.2 13.0 %copy-start = (f32[384,128]{1,0:T(8,128)S(1)}, f32[384,128]{1,0:T(8,128)}, u32[]{:S(2)}) copy-start(f32[384,128]{1,0:T(8,128)} %param.3) | copy-start | bytes 589828
  7.2 44.1 %all-gather.3.cloned.1.call-start = ((), (), s32[]{:S(2)}) async-start(), calls=%async_computation | async-start | bytes 1880064 | tf_op jit(solution)/shard_map/all_gather | solution.py:210
  20.1 15.8 %collective-permute-start.1 = (f32[384,128]{1,0:T(8,128)S(1)}, f32[384,128]{1,0:T(8,128)S(1)}, u32[]{:S(2)}, u32[]{:S(2)}) collective-permute-start(f32[384,128]{1,0:T(8,128)S(1)} %copy-done), channel_id=1, source_target_pairs={{0,4},{4,8},{8,12},{12,16},{16,20},{20,24},{24,28},{1,5},{5,9},{9,... | collective-permute-start | bytes 589832 | tf_op jit(solution)/shard_map/ppermute | solution.py:195
  27.5 8.5 %collective-permute-start = (f32[128,128]{1,0:T(8,128)S(1)}, f32[128,128]{1,0:T(8,128)S(1)}, u32[]{:S(2)}, u32[]{:S(2)}) collective-permute-start(f32[128,128]{1,0:T(8,128)S(1)} %slice.18), channel_id=1, source_target_pairs={{0,8},{4,12},{8,16},{12,20},{16,24},{20,28},{1,9},{5,13},{9,17},{1... | collective-permute-start | bytes 196616 | tf_op jit(solution)/shard_map/ppermute | solution.py:195
  30.6 5.3 %collective-permute-start.2 = (f32[8,128]{1,0:T(8,128)S(1)}, f32[8,128]{1,0:T(8,128)S(1)}, u32[]{:S(2)}, u32[]{:S(2)}) collective-permute-start(f32[8,128]{1,0:T(8,128)S(1)} %slice.19), channel_id=1, source_target_pairs={{4,0},{8,4},{12,8},{16,12},{20,16},{24,20},{28,24},{5,1},{9,5},{13... | collective-permute-start | bytes 12296 | tf_op jit(solution)/shard_map/ppermute | solution.py:195
Sparse Core Ops, SparseCore 0:
  20.3 31.0 all-gather.2

commit v2 on v1

--- a/solution.py
+++ b/solution.py
@@ -12,7 +12,8 @@
 
 
 def chase_kernel(blocks, half, blocks_dev, halo, piece_count, sweeps, *refs):
-    band_ref, eig_ref, band_out, eig_out = refs[:4]
+    band_ref, above_ref, eig_ref, under_ref, band_out, eig_out = refs[:6]
+    refs = refs[2:]
     d_refs = refs[4 : 5 + sweeps]
     l_refs = refs[5 + sweeps : 6 + 2 * sweeps]
     v_refs = refs[6 + 2 * sweeps : 6 + 3 * sweeps]
@@ -37,7 +38,7 @@
         start = pl.multiple_of(part * half, half)
         piece = band_ref[dev, :half, pl.ds(start, half)]
         extra = band_ref[dev, half : half + 1, pl.ds(start, half)]
-        rows = pltpu.roll(piece.T, 0, 1, stride=1, stride_axis=0)
+        rows = pltpu.roll(piece.T, 1, 1, stride=1, stride_axis=0)
         d_refs[0][slot(block)] = jnp.where(row >= col, rows, rows.T)
         l_refs[0][slot(block - 1)] = jnp.where(
             col > row, rows, jnp.where(eye, jnp.broadcast_to(extra, (half, half)), 0.0)
@@ -136,8 +137,9 @@
 
     device = lax.axis_index("band")
     base = device * blocks_dev - halo
-    eig = [eig_ref[e * half : (e + 1) * half, :] for e in range(halo + blocks_dev)]
-    eig.append(eig_ref[(halo + blocks_dev) * half : (halo + blocks_dev) * half + 8, :])
+    eig = [above_ref[e * half : (e + 1) * half, :] for e in range(halo)]
+    eig += [eig_ref[e * half : (e + 1) * half, :] for e in range(blocks_dev)]
+    eig.append(under_ref[...])
     for s in reversed(range(sweeps)):
         lead_rows = s + 1
         for e in range(sweeps - 1 - s + halo - sweeps, halo + blocks_dev):
@@ -189,42 +191,166 @@
         band_out[:, m * half : (m + 1) * half] = turn_ref[pl.ds(pl.multiple_of(position, 8), piece_count), :]
 
 
-def shifted(x, axis, by):
-    peers = lax.axis_size(axis)
-    pairs = [(i, i + by) for i in range(peers) if 0 <= i + by < peers]
-    return lax.ppermute(x, axis, pairs)
+def gather_kernel(half, devices, cols, takes, rev_ref, band_ref, eig_ref, all_ref, above_ref, under_ref, sems):
+    z_send, z_recv, p_send, p_recv, c_send, c_recv, e_send, e_recv, own_sem = sems
+    d, c = lax.axis_index("band"), lax.axis_index("cols")
+    count = rev_ref.shape[0]
+    full = half // count
+    pieces = full + 1
+    chips = devices // 2
+    chip, core = d // 2, d % 2
+    partner = chip * 2 + 1 - core
+
+    def at(rel):
+        return (chip + rel + chips) % chips * 2 + core
+
+    barrier = pltpu.get_barrier_semaphore()
+    peers = [(d, (c + i) % cols) for i in range(1, cols)]
+    peers += [(at(i), c) for i in range(1, chips)]
+    peers.append((partner, c))
+    for hop in range(1, len(takes) + 1):
+        peers += [((d + hop) % devices, c), ((d - hop + devices) % devices, c)]
+    for peer in peers:
+        pl.semaphore_signal(barrier, inc=1, device_id=peer, device_id_type=pl.DeviceIdType.MESH)
+    pl.semaphore_wait(barrier, len(peers))
+
+    def send(src, dst, send_sem, recv_sem, device):
+        return pltpu.make_async_remote_copy(
+            src_ref=src,
+            dst_ref=dst,
+            send_sem=send_sem,
+            recv_sem=recv_sem,
+            device_id=device,
+            device_id_type=pl.DeviceIdType.MESH,
+        )
+
+    def place(dev, p):
+        if p < full:
+            return all_ref.at[dev, pl.ds(half - (p + 1) * count, count)]
+        return all_ref.at[dev, pl.ds(half, 8)]
+
+    def source(p):
+        return rev_ref if p < full else band_ref.at[pl.ds(0, 8)]
+
+    def along(p, i):
+        return send(source(p), place(d, p), z_send.at[p, i], z_recv.at[p], (d, (c + i) % cols))
+
+    def across(p, i, src):
+        return send(src, place(d, p), p_send.at[p, i], p_recv.at[p, i], (at(i), c))
+
+    def pair(p, i, src, dev):
+        return send(src, place(dev, p), c_send.at[p, i], c_recv.at[p, i], (partner, c))
+
+    def own(p):
+        return pltpu.make_async_copy(source(p), place(d, p), own_sem)
+
+    rows_dev = eig_ref.shape[0]
+    total = sum(takes)
+    halos = []
+    end = total
+    for hop, take in enumerate(takes, 1):
+        halos.append(
+            send(
+                eig_ref.at[pl.ds(rows_dev - take, take)],
+                above_ref.at[pl.ds(end - take, take)],
+                e_send.at[hop],
+                e_recv.at[hop],
+                ((d + hop) % devices, c),
+            )
+        )
+        end -= take
+    halos.append(
+        send(eig_ref.at[pl.ds(0, 8)], under_ref, e_send.at[0], e_recv.at[0], ((d - 1 + devices) % devices, c))
+    )
+
+    for p in range(pieces):
+
+        @pl.when(c == p)
+        def _():
+            for i in range(1, cols):
+                along(p, i).start()
+            for i in range(1, chips):
+                across(p, i, source(p)).start()
+            pair(p, 0, source(p), d).start()
+            own(p).start()
+
+    for p in range(pieces):
+
+        @pl.when(c != p)
+        def _():
+            along(p, 1).wait_recv()
+            for i in range(1, chips):
+                across(p, i, place(d, p)).start()
+            pair(p, 0, place(d, p), d).start()
+
+    for halo in halos:
+        halo.start()
+    for i in range(1, chips):
+        for p in range(pieces):
+            across(p, i, place(d, p)).wait_recv()
+            pair(p, i, place(at(-i), p), at(-i)).start()
+    for p in range(pieces):
+
+        @pl.when(c == p)
+        def _():
+            own(p).wait()
+            for i in range(1, cols):
+                along(p, i).wait_send()
+
+    for p in range(pieces):
+        for i in range(1, chips):
+            across(p, i, place(d, p)).wait_send()
+        for i in range(chips):
+            pair(p, i, place(at(-i), p), at(-i)).wait()
+    for halo in halos:
+        halo.wait()
 
 
 def body(band_diagonals, eigenvectors):
     piece_count, rows_dev = band_diagonals.shape
-    double = piece_count * lax.axis_size("cols")
+    cols = lax.axis_size("cols")
+    double = piece_count * cols
     half = double // 2
     blocks_dev = rows_dev // half
     devices = lax.axis_size("band")
     blocks = blocks_dev * devices
     sweeps = SWEEPS
-    pieces = lax.all_gather(band_diagonals, "cols", axis=0, tiled=True)
-    turned = jnp.concatenate(
-        [pieces[:1], pieces[half - 1 : 0 : -1], pieces[half : half + 8]], axis=0
-    )
-    band = lax.all_gather(turned, "band", axis=0, tiled=False)
-
     halo = sweeps
-    parts = []
-    need = halo * half
-    hop = 1
-    while need > 0:
-        take = min(need, rows_dev)
-        parts.insert(0, shifted(eigenvectors[rows_dev - take :], "band", hop))
-        need -= take
-        hop += 1
-    parts.append(eigenvectors)
-    parts.append(shifted(eigenvectors[:8], "band", -1))
-    eig = jnp.concatenate(parts, axis=0)
     columns = eigenvectors.shape[1]
+    f32 = jnp.float32
+    vmem = pl.BlockSpec(memory_space=pltpu.VMEM)
+
+    takes = []
+    while sum(takes) < halo * half:
+        takes.append(min(halo * half - sum(takes), rows_dev))
+    pieces = half // piece_count + 1
+    dma = pltpu.SemaphoreType.DMA
+    band, above, under = pl.pallas_call(
+        functools.partial(gather_kernel, half, devices, cols, takes),
+        out_shape=(
+            jax.ShapeDtypeStruct((devices, half + 8, rows_dev), f32),
+            jax.ShapeDtypeStruct((halo * half, columns), f32),
+            jax.ShapeDtypeStruct((8, columns), f32),
+        ),
+        in_specs=[vmem] * 3,
+        out_specs=(vmem,) * 3,
+        scratch_shapes=[
+            [
+                dma((pieces, cols)),
+                dma((pieces,)),
+                dma((pieces, devices)),
+                dma((pieces, devices)),
+                dma((pieces, devices)),
+                dma((pieces, devices)),
+                dma((len(takes) + 1,)),
+                dma((len(takes) + 1,)),
+                dma,
+            ]
+        ],
+        compiler_params=pltpu.CompilerParams(collective_id=0, has_side_effects=True),
+    )(band_diagonals[::-1], band_diagonals, eigenvectors)
 
     slots = blocks + 3
-    f32 = jnp.float32
     scratch = (
         [pltpu.VMEM((slots, half, half), f32)] * (2 * (sweeps + 1))
         + [pltpu.VMEM((slots, half, half), f32)] * sweeps
@@ -236,18 +362,17 @@
             pltpu.VMEM((double, half), f32),
         ]
     )
-    vmem = pl.BlockSpec(memory_space=pltpu.VMEM)
     return pl.pallas_call(
         functools.partial(chase_kernel, blocks, half, blocks_dev, halo, piece_count, sweeps),
         out_shape=(
             jax.ShapeDtypeStruct((piece_count, rows_dev), f32),
             jax.ShapeDtypeStruct((rows_dev, columns), f32),
         ),
-        in_specs=[vmem, vmem],
+        in_specs=[vmem] * 4,
         out_specs=(vmem, vmem),
         scratch_shapes=scratch,
         compiler_params=pltpu.CompilerParams(vmem_limit_bytes=62 * 1024 * 1024),
-    )(band, eig)
+    )(band, above, eigenvectors, under)
 
 
 def solution(mesh):

time: 86.7 us -> 58.7 us (0.68); the launches traced: 85.1 us -> 58.4 us
  Pallas kernels: 26.9 us -> 55.5 us
  waiting for transfers between devices: 18 us -> 0 us
  between operations: 14.1 us -> 0.64 us
  starting transfers between devices: 12.4 us -> 0 us
  blocking collectives: 12 us -> 0 us
  local copies, waits for them, and re-layouts: 0.18 us -> 2.17 us
  other arithmetic: 1.5 us -> 0 us
    pallas_call x0 -> x1, Pallas kernels: none -> 28.6 us  [body(): pl.pallas_call(functools.partial(gather_kernel, half, devices, cols, take...]
    all_gather x1 -> x0, waiting for transfers between devices: 14.6 us -> none  [body(): band = lax.all_gather(turned, 'band', axis=0, tiled=False)]
    ppermute x3 -> x0, starting transfers between devices: 12.3 us -> none  [shifted(): return lax.ppermute(x, axis, pairs)]
    all_gather x1 -> x0, blocking collectives: 12 us -> none  [body(): pieces = lax.all_gather(band_diagonals, 'cols', axis=0, tiled=True)]
    ppermute x3 -> x0, waiting for transfers between devices: 3.41 us -> none  [shifted(): return lax.ppermute(x, axis, pairs)]
    rev x1, local copies, waits for them, and re-layouts: 0.15 us -> 2.17 us  [body(): band_diagonals[::-1]]
    concatenate x2 -> x0, other arithmetic: 1.5 us -> none  [the longest x1 0.8 us: body(): eig = jnp.concatenate(parts, axis=0)]
  transfers between devices with their start and end apart: 4 -> 0, of which waited for: 2 -> 0; matrix products, arithmetic and copies ran while one was open for 1% -> 0% of each run, Pallas kernels for 0% -> 0%
where the time goes in v2:
time: 58.7 us; the launch traced here: 58.4 us
  Pallas kernels  55.5 us (95%)
  local copies, waits for them, and re-layouts  2.17 us (4%)
  between operations  0.64 us (1%)
    pallas_call x1, Pallas kernels, body(): pl.pallas_call(functools.partial(gather_kernel, half, devices, cols, take...  28.6 us
    pallas_call x1, Pallas kernels, body(): pl.pallas_call(functools.partial(chase_kernel, blocks, half, blocks_dev,...  27 us
    rev x1, local copies, waits for them, and re-layouts, body(): band_diagonals[::-1]  2.17 us

profile of v2, /device:TPU:25, one launch (start us, length us, event | category | flops | bytes accessed | tf_op | source)
XLA Modules:
  0.0 58.4 jit_solution(9230782222809897297)
XLA Ops:
  0.6 2.2 %rev.3.rev_ref = f32[64,384]{1,0:T(8,128)} reverse(f32[64,384]{1,0:T(8,128)} %band_ref.1), dimensions={0} | reverse | bytes 196608 | tf_op jit(solution)/shard_map/rev | solution.py:351
  2.8 28.6 %shard_map.41 = (f32[8,136,384]{2,1,0:T(8,128)}, f32[512,128]{1,0:T(8,128)}, f32[8,128]{1,0:T(8,128)}) custom-call(f32[64,384]{1,0:T(8,128)} %rev.3.rev_ref, f32[64,384]{1,0:T(8,128)} %band_ref.1, f32[384,128]{1,0:T(8,128)} %refs_2_.1), custom_call_target="tpu_custom_call" | custom-call | tf_op jit(solution)/shard_map/pallas_call | solution.py:328
  31.4 27.0 %shard_map.42 = (f32[64,384]{1,0:T(8,128)}, f32[384,128]{1,0:T(8,128)}) custom-call(f32[8,136,384]{2,1,0:T(8,128)} %get-tuple-element.5.refs_0_, f32[512,128]{1,0:T(8,128)} %get-tuple-element.6.refs_1_, f32[384,128]{1,0:T(8,128)} %refs_2_.1, f32[8,128]{1,0:T(8,128)} %get-tuple-element.7.refs_3_), custom_call_target="tpu_custom_call" | custom-call | tf_op jit(solution)/shard_map/pallas_call | solution.py:365

commit v3 on v2

--- a/solution.py
+++ b/solution.py
@@ -191,28 +191,43 @@
         band_out[:, m * half : (m + 1) * half] = turn_ref[pl.ds(pl.multiple_of(position, 8), piece_count), :]
 
 
-def gather_kernel(half, devices, cols, takes, rev_ref, band_ref, eig_ref, all_ref, above_ref, under_ref, sems):
+def gather_kernel(half, devices, cols, takes, band_ref, eig_ref, all_ref, above_ref, under_ref, rev_ref, sems):
     z_send, z_recv, p_send, p_recv, c_send, c_recv, e_send, e_recv, own_sem = sems
     d, c = lax.axis_index("band"), lax.axis_index("cols")
-    count = rev_ref.shape[0]
+    count = band_ref.shape[0]
     full = half // count
     pieces = full + 1
     chips = devices // 2
+    tall = chips // 2
     chip, core = d // 2, d % 2
     partner = chip * 2 + 1 - core
+    spot = (1 - chip % 2) * (chip // 2) + (chip % 2) * (chips - 1 - chip // 2)
 
     def at(rel):
-        return (chip + rel + chips) % chips * 2 + core
+        ring = (spot + rel + chips) % chips
+        turn = ring // tall
+        return ((1 - turn) * 2 * ring + turn * (2 * (chips - 1 - ring) + 1)) * 2 + core
+
+    for r in range(count):
+        rev_ref[r : r + 1, :] = band_ref[count - 1 - r : count - r, :]
 
     barrier = pltpu.get_barrier_semaphore()
-    peers = [(d, (c + i) % cols) for i in range(1, cols)]
-    peers += [(at(i), c) for i in range(1, chips)]
-    peers.append((partner, c))
+    peers = [(at(1), c), (at(-1), c), (partner, c)]
     for hop in range(1, len(takes) + 1):
         peers += [((d + hop) % devices, c), ((d - hop + devices) % devices, c)]
     for peer in peers:
         pl.semaphore_signal(barrier, inc=1, device_id=peer, device_id_type=pl.DeviceIdType.MESH)
-    pl.semaphore_wait(barrier, len(peers))
+
+    @pl.when(c > 0)
+    def _():
+        pl.semaphore_signal(barrier, inc=1, device_id=(d, c - 1), device_id_type=pl.DeviceIdType.MESH)
+
+    @pl.when(c < cols - 1)
+    def _():
+        pl.semaphore_signal(barrier, inc=1, device_id=(d, c + 1), device_id_type=pl.DeviceIdType.MESH)
+
+    beside = (c + cols - 1) // cols + 1 - (c + 1) // cols
+    pl.semaphore_wait(barrier, len(peers) + beside)
 
     def send(src, dst, send_sem, recv_sem, device):
         return pltpu.make_async_remote_copy(
@@ -224,30 +239,56 @@
             device_id_type=pl.DeviceIdType.MESH,
         )
 
-    def place(dev, p):
-        if p < full:
-            return all_ref.at[dev, pl.ds(half - (p + 1) * count, count)]
-        return all_ref.at[dev, pl.ds(half, 8)]
+    def rows_of(p, part):
+        first, size = (half - (p + 1) * count, count) if p < full else (half, 8)
+        if part is not None and p < full:
+            first, size = first + part * (size // 2), size // 2
+        return pl.ds(first, size)
+
+    def place(dev, p, part=None):
+        return all_ref.at[dev, rows_of(p, part)]
 
     def source(p):
         return rev_ref if p < full else band_ref.at[pl.ds(0, 8)]
 
-    def along(p, i):
-        return send(source(p), place(d, p), z_send.at[p, i], z_recv.at[p], (d, (c + i) % cols))
-
-    def across(p, i, src):
-        return send(src, place(d, p), p_send.at[p, i], p_recv.at[p, i], (at(i), c))
-
-    def pair(p, i, src, dev):
-        return send(src, place(dev, p), c_send.at[p, i], c_recv.at[p, i], (partner, c))
+    def along(p, up, src):
+        to = (c + 1) % cols if up else (c - 1 + cols) % cols
+        return send(src, place(d, p), z_send.at[p, int(up)], z_recv.at[p], (d, to))
+
+    def hops(p):
+        for j in range(1, chips // 2 + 1):
+            for way in (1, -1):
+                if 2 * j < chips:
+                    yield j, way, None
+                elif p < full:
+                    yield j, way, 0 if way == 1 else 1
+                elif way == 1:
+                    yield j, way, None
+
+    def across(p, j, way, part, src=None):
+        dev = at(-way * (j - 1))
+        src = place(dev, p, part) if src is None else src
+        which = 2 * j + (way + 1) // 2
+        return send(src, place(dev, p, part), p_send.at[p, which], p_recv.at[p, which], (at(way), c))
+
+    def pair(p, j, way, part, src=None):
+        dev = at(-way * j)
+        src = place(dev, p, part) if src is None else src
+        which = 2 * j + (way + 1) // 2
+        return send(src, place(dev, p, part), c_send.at[p, which], c_recv.at[p, which], (partner, c))
 
     def own(p):
         return pltpu.make_async_copy(source(p), place(d, p), own_sem)
 
+    def first_hops(p, src):
+        for j, way, part in hops(p):
+            if j == 1:
+                across(p, 1, way, part, src).start()
+        pair(p, 0, 1, None, src).start()
+
     rows_dev = eig_ref.shape[0]
-    total = sum(takes)
     halos = []
-    end = total
+    end = sum(takes)
     for hop, take in enumerate(takes, 1):
         halos.append(
             send(
@@ -267,41 +308,66 @@
 
         @pl.when(c == p)
         def _():
-            for i in range(1, cols):
-                along(p, i).start()
-            for i in range(1, chips):
-                across(p, i, source(p)).start()
-            pair(p, 0, source(p), d).start()
+            @pl.when(c < cols - 1)
+            def _():
+                along(p, True, source(p)).start()
+
+            @pl.when(c > 0)
+            def _():
+                along(p, False, source(p)).start()
+
+            first_hops(p, source(p))
             own(p).start()
 
-    for p in range(pieces):
-
+    def receive(p):
         @pl.when(c != p)
         def _():
-            along(p, 1).wait_recv()
-            for i in range(1, chips):
-                across(p, i, place(d, p)).start()
-            pair(p, 0, place(d, p), d).start()
-
+            along(p, True, place(d, p)).wait_recv()
+
+            @pl.when((c > p) & (c < cols - 1))
+            def _():
+                along(p, True, place(d, p)).start()
+
+            @pl.when((c < p) & (c > 0))
+            def _():
+                along(p, False, place(d, p)).start()
+
+            first_hops(p, place(d, p))
+
+    def relay(p, level):
+        for j, way, part in hops(p):
+            if j == level:
+                across(p, j, way, part).wait_recv()
+                for j2, way2, part2 in hops(p):
+                    if j2 == j + 1 and way2 == way:
+                        across(p, j2, way, part2).start()
+                pair(p, j, way, part).start()
+
+    for p in reversed(range(pieces)):
+        receive(p)
     for halo in halos:
         halo.start()
-    for i in range(1, chips):
-        for p in range(pieces):
-            across(p, i, place(d, p)).wait_recv()
-            pair(p, i, place(at(-i), p), at(-i)).start()
+    for level in range(1, chips // 2 + 1):
+        for p in reversed(range(pieces)):
+            relay(p, level)
     for p in range(pieces):
 
         @pl.when(c == p)
         def _():
             own(p).wait()
-            for i in range(1, cols):
-                along(p, i).wait_send()
-
-    for p in range(pieces):
-        for i in range(1, chips):
-            across(p, i, place(d, p)).wait_send()
-        for i in range(chips):
-            pair(p, i, place(at(-i), p), at(-i)).wait()
+
+        @pl.when((c >= p) & (c < cols - 1))
+        def _():
+            along(p, True, place(d, p)).wait_send()
+
+        @pl.when((c <= p) & (c > 0))
+        def _():
+            along(p, False, place(d, p)).wait_send()
+
+        for j, way, part in hops(p):
+            across(p, j, way, part).wait_send()
+            pair(p, j, way, part).wait()
+        pair(p, 0, 1, None).wait()
     for halo in halos:
         halo.wait()
 
@@ -332,23 +398,24 @@
             jax.ShapeDtypeStruct((halo * half, columns), f32),
             jax.ShapeDtypeStruct((8, columns), f32),
         ),
-        in_specs=[vmem] * 3,
+        in_specs=[vmem] * 2,
         out_specs=(vmem,) * 3,
         scratch_shapes=[
+            pltpu.VMEM((piece_count, rows_dev), f32),
             [
-                dma((pieces, cols)),
+                dma((pieces, 2)),
                 dma((pieces,)),
-                dma((pieces, devices)),
-                dma((pieces, devices)),
-                dma((pieces, devices)),
-                dma((pieces, devices)),
+                dma((pieces, devices + 2)),
+                dma((pieces, devices + 2)),
+                dma((pieces, devices + 2)),
+                dma((pieces, devices + 2)),
                 dma((len(takes) + 1,)),
                 dma((len(takes) + 1,)),
                 dma,
             ]
         ],
         compiler_params=pltpu.CompilerParams(collective_id=0, has_side_effects=True),
-    )(band_diagonals[::-1], band_diagonals, eigenvectors)
+    )(band_diagonals, eigenvectors)
 
     slots = blocks + 3
     scratch = (

time: 58.7 us -> 55 us (0.937)
  local copies, waits for them, and re-layouts: 2.17 us -> 0 us
  Pallas kernels: 55.5 us -> 54.2 us
    rev x1 -> x0, local copies, waits for them, and re-layouts: 2.17 us -> none  [body(): band_diagonals[::-1]]
    pallas_call x1, Pallas kernels: 28.6 us -> 27.3 us  [body(): pl.pallas_call(functools.partial(gather_kernel, half, devices, cols, take...]
where the time goes in v3:
time: 55 us; the launch traced here: 54.9 us
  Pallas kernels  54.2 us (99%)
  between operations  0.64 us (1%)
    pallas_call x1, Pallas kernels, body(): pl.pallas_call(functools.partial(gather_kernel, half, devices, cols, take...  27.3 us
    pallas_call x1, Pallas kernels, body(): pl.pallas_call(functools.partial(chase_kernel, blocks, half, blocks_dev,...  27 us

profile of v3, /device:TPU:25, one launch (start us, length us, event | category | flops | bytes accessed | tf_op | source)
XLA Modules:
  0.0 54.9 jit_solution(16473501939816969051)
XLA Ops:
  0.6 27.3 %shard_map.41 = (f32[8,136,384]{2,1,0:T(8,128)}, f32[512,128]{1,0:T(8,128)}, f32[8,128]{1,0:T(8,128)}) custom-call(f32[64,384]{1,0:T(8,128)} %band_ref.1, f32[384,128]{1,0:T(8,128)} %refs_2_.1), custom_call_target="tpu_custom_call" | custom-call | tf_op jit(solution)/shard_map/pallas_call | solution.py:394
  27.9 27.0 %shard_map.42 = (f32[64,384]{1,0:T(8,128)}, f32[384,128]{1,0:T(8,128)}) custom-call(f32[8,136,384]{2,1,0:T(8,128)} %get-tuple-element.5.refs_0_, f32[512,128]{1,0:T(8,128)} %get-tuple-element.6.refs_1_, f32[384,128]{1,0:T(8,128)} %refs_2_.1, f32[8,128]{1,0:T(8,128)} %get-tuple-element.7.refs_3_), custom_call_target="tpu_custom_call" | custom-call | tf_op jit(solution)/shard_map/pallas_call | solution.py:432
